TPU v7x, 32 devices: a whole 2x2x4 slice. The times are simulated.
32 devices in a mesh: samples: 16 (over z, y, core), feat: 2 (over x).
Axes of the slice: x: 2, y: 2, z: 4, core: 2. Of those that a mesh axis runs over, the one named last changes fastest.
Arguments:
- samples: float32 [4096, 4096], P('samples', 'feat'), may hold values from -12 to 12, as said below
- factor: float32 [4096, 512], P('feat'), may hold values from -6 to 6
Outputs:
- new_factor: float32 [4096, 512], P('feat')
Inputs may be any that keep to these rules, and one draw needn't show every extreme that they name: `samples`: Real-valued data.
All inputs are finite; a program needn't handle non-finite values.
Results may differ from a plain program's by a relative error of at most 0.00007.
Values sent between devices are 32-bit elements; how exact they have to be, the bound alone decides.
No kernel may reach another device: no remote copies, remote signals or barrier semaphores. Data moves between devices by JAX's collectives and lax.ppermute only.
A program may use at most 64 MiB of HBM per device.

v0:
```python
import jax
import jax.numpy as jnp
from jax import lax
from jax.sharding import PartitionSpec as P

D = 4096
R = 512


def per_device(samples, factor):
    high = lax.Precision.HIGHEST
    contract_rows = (((0,), (0,)), ((), ()))
    scaled = factor * (1.0 / jnp.sqrt(jnp.float32(D)))
    local_proj = jnp.dot(samples, scaled, precision=high, preferred_element_type=jnp.float32)
    proj = lax.psum(local_proj, "feat")
    squared = proj * proj
    rows_total = samples.shape[0] * lax.axis_size("samples")
    half_gram = lax.dot_general(
        scaled, scaled, contract_rows, precision=high, preferred_element_type=jnp.float32
    )
    gram = lax.psum(half_gram, "feat")
    squared_gram = gram * gram
    coef = 6.0 / jnp.sqrt(jnp.float32(D))
    local_moment = lax.dot_general(
        samples, squared, contract_rows, precision=high, preferred_element_type=jnp.float32
    )
    moment = lax.psum(local_moment, "samples") / rows_total
    gram_term = jnp.dot(scaled, squared_gram, precision=high, preferred_element_type=jnp.float32)
    grad = coef * (gram_term - moment)
    total = lax.psum(jnp.sum(grad * grad), "feat")
    rms = jnp.sqrt(total / (D * R)) + 1e-06
    return factor - 0.5 * grad / rms


def solution(mesh):
    placed = (P("samples", "feat"), P("feat", None))
    return jax.shard_map(
        per_device, mesh=mesh, in_specs=placed, out_specs=P("feat", None), check_vma=False
    )
```

profile of v0, /device:TPU:0, one launch (start us, length us, event | category | flops | bytes accessed | tf_op | source)
XLA Modules:
  0.0 228.2 jit_solution(14365884169956142107)
XLA Ops:
  6.5 0.0 copy-start
  6.5 0.0 all-reduce.6.cloned.1.call-start
  6.5 0.0 copy-start.1
  6.5 11.3 %fusion.4 = f32[512,512]{1,0:T(8,128)} fusion(f32[2048,512]{1,0:T(8,128)} %param.3), kind=kOutput, calls=%fused_computation.7 | convolution fusion | flops 6443499520 | bytes 5242880 | tf_op jit(solution)/shard_map/dot_general | solution.py:18
  17.8 0.0 copy-done
  17.8 0.0 copy-done.1
  17.9 7.5 %fusion.11 = f32[256,512]{0,1:T(8,128)} fusion(f32[256,2048]{1,0:T(8,128)S(1)} %copy-done, f32[2048,512]{1,0:T(8,128)S(1)} %copy-done.1), kind=kOutput, calls=%fused_computation.13 | convolution fusion | flops 3222274048 | bytes 6815744 | tf_op jit(solution)/shard_map/dot_general | solution.py:14
  25.4 0.0 all-reduce.6.cloned.1.call-update
  25.4 0.2 all-reduce.4.cloned.1.call-start
  25.6 54.2 %all-reduce.6.cloned.1.call-done = (f32[256,512]{0,1:T(8,128)}, f32[512,512]{1,0:T(8,128)}) async-done(((f32[256,512]{0,1:T(8,128)}, f32[512,512]{1,0:T(8,128)}), (f32[256,512]{0,1:T(8,128)}, f32[512,512]{1,0:T(8,128)})) %all-reduce.6.cloned.1.call-update) | async-done | bytes 1572880 | tf_op jit(solution)/shard_map/psum | solution.py:15
  79.8 6.1 %convolution_bitcast_fusion = f32[2048,512]{1,0:T(8,128)} fusion(f32[256,2048]{1,0:T(8,128)S(1)} %copy-done, f32[256,512]{0,1:T(8,128)} %get-tuple-element.5), kind=kOutput, calls=%fused_computation.9 | convolution fusion | flops 3221356544 | bytes 6815744 | tf_op jit(solution)/shard_map/dot_general | solution.py:24
  86.0 0.0 copy-start.2
  86.0 0.0 all-reduce.4.cloned.1.call-update
  86.0 111.2 %all-reduce.4.cloned.1.call-done = f32[2048,512]{1,0:T(8,128)} async-done(((f32[2048,512]{1,0:T(8,128)}), f32[2048,512]{1,0:T(8,128)}) %all-reduce.4.cloned.1.call-update) | async-done | bytes 4194320 | tf_op jit(solution)/shard_map/psum | solution.py:27
  197.2 0.0 copy-done.2
  197.2 11.5 %multiply_reduce_fusion = (f32[]{:T(128)}, f32[2048,512]{1,0:T(8,128)}) fusion(f32[2048,512]{1,0:T(8,128)} %all-reduce.4.cloned.1.call-done, f32[512,512]{1,0:T(8,128)S(1)} %copy-done.2, f32[2048,512]{1,0:T(8,128)} %param.3), kind=kOutput, calls=%fused_computation.1 | convolution fusion | flops 6449004544 | bytes 13631492 | tf_op jit(solution)/shard_map/dot_general | solution.py:28
  208.7 5.5 %psum.31 = f32[]{:T(128)} all-reduce(f32[]{:T(128)} %get-tuple-element.7), channel_id=1, replica_groups=mesh['samples'=16,'feat'=2] {'feat'}, use_global_device_ids=true, to_apply=%region_4.0 | all-reduce | flops 1 | bytes 8 | tf_op jit(solution)/shard_map/psum | solution.py:30
  214.9 6.5 %divide_subtract_fusion = f32[2048,512]{1,0:T(8,128)} fusion(f32[2048,512]{1,0:T(8,128)} %param.3, f32[2048,512]{1,0:T(8,128)} %get-tuple-element.8, f32[]{:T(128)S(6)} %add.11), kind=kLoop, calls=%fused_computation | loop fusion | flops 3145728 | bytes 12582916 | tf_op jit(solution)/shard_map/sub | solution.py:32
Async XLA Ops:
  6.5 11.3 %copy-start = (f32[256,2048]{1,0:T(8,128)S(1)}, f32[256,2048]{1,0:T(8,128)}, u32[]{:S(2)}) copy-start(f32[256,2048]{1,0:T(8,128)} %param.2) | copy-start | bytes 6291460
  6.5 73.3 %all-reduce.6.cloned.1.call-start = ((), (), s32[]{:S(2)}) async-start(), calls=%async_computation.1 | async-start | bytes 3145728 | tf_op jit(solution)/shard_map/psum | solution.py:15
  6.5 11.3 %copy-start.1 = (f32[2048,512]{1,0:T(8,128)S(1)}, f32[2048,512]{1,0:T(8,128)}, u32[]{:S(2)}) copy-start(f32[2048,512]{1,0:T(8,128)} %param.3) | copy-start | bytes 12582916
  25.4 171.8 %all-reduce.4.cloned.1.call-start = ((), (), s32[]{:S(2)}) async-start(), calls=%async_computation | async-start | bytes 8388608 | tf_op jit(solution)/shard_map/psum | solution.py:27
  86.0 111.2 %copy-start.2 = (f32[512,512]{1,0:T(8,128)S(1)}, f32[512,512]{1,0:T(8,128)}, u32[]{:S(2)}) copy-start(f32[512,512]{1,0:T(8,128)} %get-tuple-element.6) | copy-start | bytes 3145732
Sparse Core Ops, SparseCore 0:
  25.5 54.2 all-reduce.5
  86.1 111.0 all-reduce.3
where the time goes:
time: 228 us
  waiting for transfers between devices  165 us (72%)
  matrix products  36.5 us (16%)
  between operations  14 us (6%)
  other arithmetic  6.53 us (3%)
  blocking collectives  5.53 us (2%)
    psum x1, waiting for transfers between devices, per_device(): moment = lax.psum(local_moment, 'samples') / rows_total  111 us
    psum x1, waiting for transfers between devices, per_device(): proj = lax.psum(local_proj, 'feat')  54.2 us
    dot_general x1, matrix products, per_device(): jnp.dot(scaled, squared_gram, precision=high, preferred_element_type=jnp....  11.5 us
    dot_general x1, matrix products, per_device(): lax.dot_general(scaled, scaled, contract_rows, precision=high, preferred_...  11.3 us
    dot_general x1, matrix products, per_device(): jnp.dot(samples, scaled, precision=high, preferred_element_type=jnp.float32)  7.54 us
    sub x1, other arithmetic, per_device(): return factor - 0.5 * grad / rms  6.53 us
    dot_general x1, matrix products, per_device(): lax.dot_general(samples, squared, contract_rows, precision=high, preferre...  6.14 us
    psum x1, blocking collectives, per_device(): total = lax.psum(jnp.sum(grad * grad), 'feat')  5.53 us
  transfers between devices with their start and end apart: 2, of which 2 were waited for; matrix products, arithmetic and copies ran while one was open for 0% of the time, Pallas kernels for 0%

commit v1 on v0

v1 whole, which is shorter than its diff:
```python
import functools

import jax
import jax.numpy as jnp
from jax import lax
from jax.experimental import pallas as pl
from jax.experimental.pallas import tpu as pltpu
from jax.sharding import PartitionSpec as P


TILE = (8, 128)
CHUNKS = 4
WIDE, NARROW = jnp.float32, jnp.bfloat16


def after(x, *first):
    return lax.optimization_barrier((x,) + first)[0]


def position():
    me = lax.axis_index("samples")
    return me & 1, (me >> 1) & 1, me >> 2


def block(index, size):
    return pl.ds(pl.multiple_of(index * size, size), size)


def split(x):
    high = x.astype(NARROW)
    return high, (x - high.astype(WIDE)).astype(NARROW)


def matmul(a, b, contract=((1,), (0,))):
    return lax.dot_general(a, b, (contract, ((), ())), preferred_element_type=WIDE)


def three_pass(a_high, a_low, pair):
    cols = pair.shape[1] // 2
    wide = matmul(a_high, pair)
    return wide[:, :cols] + (wide[:, cols:] + matmul(a_low, pair[:, :cols]))


def fetch(source, held, sem):
    copy = pltpu.make_async_copy(source, held, sem)
    copy.start()
    return copy


def own_kernel(kept, samples_ref, factor_ref, proj_ref, pair_ref, *refs):
    *more, held_x, held_f, sem = refs
    core, y, _ = position()
    cols = held_f.shape[1]
    here = block(2 * core + (y if kept else 1 - y), cols)
    step = held_x.shape[1] // CHUNKS
    copies = []
    for n in range(CHUNKS):
        part = pl.ds(n * step, step)
        copies.append(fetch(factor_ref.at[part, here], held_f.at[part], sem.at[0, n]))
        copies.append(fetch(samples_ref.at[:, part], held_x.at[:, part], sem.at[1, n]))
    total = None
    for n in range(CHUNKS):
        part = pl.ds(n * step, step)
        copies[2 * n].wait()
        f = held_f[part]
        pair = jnp.concatenate(split(f), axis=1)
        pair_ref[part] = pair
        copies[2 * n + 1].wait()
        x = held_x[:, part]
        add = three_pass(*split(x), pair)
        total = add if total is None else total + add
        if kept:
            high_ref, low_ref, turned_ref = more
            high_ref[part], low_ref[part] = split(x.T)
            turned_ref[:cols, part], turned_ref[cols:, part] = split(f.T)
    proj_ref[...] = total


def other_kernel(samples_ref, pair_ref, proj_ref, held_x, sem):
    step = held_x.shape[1] // CHUNKS
    parts = [pl.ds(n * step, step) for n in range(CHUNKS)]
    copies = [
        fetch(samples_ref.at[:, part], held_x.at[:, part], sem.at[n])
        for n, part in enumerate(parts)
    ]
    total = None
    for part, copy in zip(parts, copies):
        copy.wait()
        add = three_pass(*split(held_x[:, part]), pair_ref[part])
        total = add if total is None else total + add
    proj_ref[...] = total


def both_kernel(samples_ref, pair_ref, own_ref, both_ref, high_ref, low_ref, held_x, sem):
    step = held_x.shape[1] // CHUNKS
    parts = [pl.ds(n * step, step) for n in range(CHUNKS)]
    copies = [
        fetch(samples_ref.at[:, part], held_x.at[:, part], sem.at[n])
        for n, part in enumerate(parts)
    ]
    count = own_ref.shape[0]
    both_ref[:count] = own_ref[...]
    total = None
    for part, copy in zip(parts, copies):
        copy.wait()
        x = held_x[:, part]
        add = three_pass(*split(x), pair_ref[part])
        total = add if total is None else total + add
        high_ref[part], low_ref[part] = split(x.T)
    both_ref[count:] = total


def moment_kernel(scale, starts, k, *refs):
    *projs, own_h, own_l, oth_h, oth_l, out_ref = refs
    rows, count = out_ref.shape[0], own_h.shape[1]
    here = block(position()[2] ^ k, rows)
    total = None
    for n, (h, l) in enumerate(((own_h, own_l), (oth_h, oth_l))):
        a, b = projs[2 * n : 2 * n + 2] if len(projs) == 4 else projs
        start = starts[n]
        proj = (a[start : start + count] + b[start : start + count]) * scale
        pair = jnp.concatenate(split(proj * proj), axis=1)
        part = three_pass(h[here, :], l[here, :], pair)
        total = part if total is None else total + part
    out_ref[...] = total


def gram_kernel(factor_ref, turned_ref, out_ref, held, sem):
    step = held.shape[0] // CHUNKS
    parts = [pl.ds(n * step, step) for n in range(CHUNKS)]
    copies = [
        fetch(factor_ref.at[part], held.at[part], sem.at[n]) for n, part in enumerate(parts)
    ]
    cols = out_ref.shape[0]
    total = None
    for part, copy in zip(parts, copies):
        copy.wait()
        high, low = split(held[part])
        tall = matmul(turned_ref[:, part], high)
        add = tall[:cols] + (tall[cols:] + matmul(turned_ref[:cols, part], low))
        total = add if total is None else total + add
    out_ref[...] = total


def term_kernel(scale, factor_ref, a_ref, b_ref, out_ref, held, sem):
    fetch(factor_ref.at[block(position()[2], held.shape[0])], held, sem).wait()
    gram = (a_ref[...] + b_ref[...]) * (scale * scale)
    cols = gram.shape[0]
    tall = jnp.concatenate(split(gram * gram), axis=0)
    high, low = split(held[...])
    nt = ((1,), (1,))
    wide = matmul(high, tall, nt)
    out_ref[...] = (
        wide[:, :cols] + (wide[:, cols:] + matmul(low, tall[:cols], nt))
    ) * scale


def grad_kernel(coef, total_rows, term_ref, *refs):
    *parts, grad_ref, sums_ref = refs
    total = parts[0][...]
    for part in parts[1:]:
        total = total + part[...]
    grad = coef * (term_ref[...] - total / total_rows)
    grad_ref[...] = grad
    down = jnp.sum(grad * grad, axis=0, keepdims=True)
    sums_ref[...] = jnp.broadcast_to(jnp.sum(down, axis=1, keepdims=True), sums_ref.shape)


def update_kernel(places, fresh, entries, rows, cols, sums_a, sums_b, factor_ref, *refs):
    count = len(places)
    blocks = refs[:count]
    out_ref, held, got, in_sem, block_sem, out_sem = refs[count + (not fresh) :]
    core, y, z = position()
    slabs = count // 4

    def slab(s):
        return block(z ^ places[4 * s][0], rows)

    loads, fetches = [], []
    for s in range(slabs):
        loads.append(fetch(factor_ref.at[slab(s)], held.at[s], in_sem.at[s]))
        for b in range(4 * s, 4 * s + 4):
            fetches.append(fetch(blocks[b], got.at[b], block_sem.at[b]))
    rms = jnp.sqrt((sums_a[...] + sums_b[...]) / entries) + 1e-06
    step = (0.5 / rms)[0:1, 0:1]
    stores = []
    for s in range(slabs):
        loads[s].wait()
        for b in range(4 * s, 4 * s + 4):
            fetches[b].wait()
            _, j, i = places[b]
            here = block(2 * (core ^ i) + (y ^ j), cols)
            held[s, :, here] = held[s, :, here] - step * got[b]
        stores.append(fetch(held.at[s], out_ref.at[slab(s)], out_sem.at[s]))
    for store in stores:
        store.wait()


def in_hbm(x):
    return pltpu.with_memory_space_constraint(x, pltpu.HBM)


VMEM, HBM = pl.BlockSpec(memory_space=pltpu.VMEM), pl.BlockSpec(memory_space=pltpu.HBM)


def update(places, sums, factor, blocks, entries, rows, cols, out=None):
    count = len(blocks)
    slabs = count // 4
    fresh = out is None
    return pl.pallas_call(
        functools.partial(update_kernel, places, fresh, entries, rows, cols),
        out_shape=jax.ShapeDtypeStruct(factor.shape, factor.dtype),
        in_specs=[VMEM, VMEM, HBM]
        + [pl.BlockSpec(memory_space=pl.ANY)] * count
        + [HBM] * (not fresh),
        out_specs=HBM,
        input_output_aliases={} if fresh else {3 + count: 0},
        scratch_shapes=[
            pltpu.VMEM((slabs, rows, factor.shape[1]), WIDE),
            pltpu.VMEM((count, rows, cols), WIDE),
            pltpu.SemaphoreType.DMA((slabs,)),
            pltpu.SemaphoreType.DMA((count,)),
            pltpu.SemaphoreType.DMA((slabs,)),
        ],
        compiler_params=pltpu.CompilerParams(vmem_limit_bytes=12 << 20),
        name="update",
    )(*sums, in_hbm(factor), *blocks, *([] if fresh else [out]))


def call(kernel, inputs, outputs, grant, hbm=(), scratch=()):
    return pl.pallas_call(
        kernel,
        out_shape=[jax.ShapeDtypeStruct(shape, kind) for shape, kind in outputs],
        in_specs=[HBM if i in hbm else VMEM for i in range(len(inputs))],
        out_specs=[VMEM] * len(outputs),
        scratch_shapes=list(scratch),
        compiler_params=pltpu.CompilerParams(vmem_limit_bytes=grant << 20),
    )(*[in_hbm(x) if i in hbm else x for i, x in enumerate(inputs)])


def low_bit(k):
    return k & -k


def step_of(samples, factor):
    features, rank = factor.shape
    count = samples.shape[0]
    n = lax.axis_size("samples")
    halves = lax.axis_size("feat")
    full = features * halves
    depth = n // 4
    rows = features // depth
    cols = rank // 4

    def swap(x, bit):
        return lax.ppermute(x, "samples", [(i, i ^ bit) for i in range(n)])

    def across(x):
        return lax.ppermute(x, "feat", [(i, (i + 1) % halves) for i in range(halves)])

    proj_of, pair_of = ((count, cols), WIDE), ((features, 2 * cols), NARROW)
    turned = ((features, count), NARROW)
    flipped = ((2 * cols, features), NARROW)
    block_of = ((rows, cols), WIDE)
    held_x = [pltpu.VMEM(samples.shape, WIDE)]
    held_f = [pltpu.VMEM((features, cols), WIDE)]
    dmas = [pltpu.SemaphoreType.DMA((CHUNKS,))]
    two_dmas = [pltpu.SemaphoreType.DMA((2, CHUNKS))]

    other = swap(samples, 1)
    own_t, pair_t = call(
        functools.partial(own_kernel, False), [samples, factor],
        [proj_of, pair_of], 12, (0, 1), held_x + held_f + two_dmas,
    )
    own_t2 = across(own_t)
    (oth_t,) = call(other_kernel, [other, pair_t], [proj_of], 10, (0,), held_x + dmas)
    oth_t2 = across(oth_t)
    own_m, pair_m, own_h, own_l, turned_m = call(
        functools.partial(own_kernel, True), [after(samples, oth_t), factor],
        [proj_of, pair_of, turned, turned, flipped], 14, (0, 1), held_x + held_f + two_dmas,
    )
    both, oth_h, oth_l = call(
        both_kernel, [other, pair_m, own_m],
        [((2 * count, cols), WIDE), turned, turned], 12, (0,), held_x + dmas,
    )
    both2 = across(both)

    def moment_of(k, projs, starts):
        return call(
            functools.partial(moment_kernel, full**-0.5, starts, k),
            [*projs, own_h, own_l, oth_h, oth_l], [block_of], 8,
        )[0]

    order = range(depth - 1, -1, -1)
    arrived, kept = {}, {}
    last = both
    for k in order:
        last = moment_of(k, [after(own_t, last), own_t2, oth_t, oth_t2], (0, 0))
        arrived[k] = swap(last, 2)
    for k in order:
        kept[k] = last = moment_of(k, [after(both, last), both2], (0, count))
    (gram,) = call(
        gram_kernel, [factor, after(turned_m, last)], [((cols, rank), WIDE)], 10, (0,),
        [pltpu.VMEM(factor.shape, WIDE)] + dmas,
    )
    (term,) = call(
        functools.partial(term_kernel, full**-0.5),
        [factor, gram, across(gram)], [block_of], 8, (0,),
        [pltpu.VMEM((rows, rank), WIDE), pltpu.SemaphoreType.DMA],
    )
    parts = {k: [kept[k], arrived[k]] for k in order}
    for k in order:
        if k:
            if k + 1 < depth:
                parts[k][1] = after(arrived[k], previous)
            previous = parts[k][0]
            for part in parts[k][1:]:
                previous = previous + part
            bit = low_bit(k)
            parts[k ^ bit].append(swap(previous, 4 * bit))
    grad, sums = call(
        functools.partial(grad_kernel, 6.0 / full**0.5, count * n),
        [term, *parts[0]], [block_of, (TILE, WIDE)], 8,
    )
    sums = sums + across(sums)
    bit = depth // 2
    while bit:
        sums = sums + swap(sums, 4 * bit)
        bit //= 2
    sums = sums + swap(sums, 2)
    sums = (sums, swap(sums, 1))

    held = {0: grad}
    bit = depth // 2
    while bit:
        for k in sorted(held):
            held[k ^ bit] = swap(held[k], 4 * bit)
        bit //= 2
    out = None
    for group in (range(depth - 1), (depth - 1,)):
        blocks, places = [], []
        for k in group:
            for j, value in enumerate((held[k], swap(held[k], 2))):
                blocks += [value, swap(value, 1)]
                places += [(k, j, 0), (k, j, 1)]
        out = update(places, sums, factor, blocks, full * rank, rows, cols, out)
    return out


def solution(mesh):
    placed = (P("samples", "feat"), P("feat", None))
    return jax.shard_map(
        step_of, mesh=mesh, in_specs=placed, out_specs=P("feat", None), check_vma=False
    )
```

time: 228 us -> 106 us (0.46)
  waiting for transfers between devices: 165 us -> 45.5 us
  matrix products: 36.5 us -> 0 us
  starting transfers between devices: 0.22 us -> 34.7 us
  Pallas kernels: 0 us -> 23.7 us
  between operations: 14 us -> 0.18 us
  other arithmetic: 6.53 us -> 0.12 us
  blocking collectives: 5.53 us -> 0 us
    psum x2 -> x0, waiting for transfers between devices: 165 us -> none  [the longest x1 111 us: per_device(): moment = lax.psum(local_moment, 'samples') / rows_total]
    ppermute x0 -> x32, waiting for transfers between devices: none -> 45.5 us  [the longest x27 39.7 us: swap(): return lax.ppermute(x, 'samples', [(i, i ^ bit) for i in range(n)])]
    dot_general x4 -> x0, matrix products: 36.5 us -> none  [the longest x1 11.5 us: per_device(): jnp.dot(scaled, squared_gram, precision=high, preferred_element_type=jnp....]
    ppermute x0 -> x32, starting transfers between devices: none -> 34.7 us  [the longest x27 26.9 us: swap(): return lax.ppermute(x, 'samples', [(i, i ^ bit) for i in range(n)])]
    pallas_call x0 -> x17, Pallas kernels: none -> 23.7 us  [the longest x15 17.9 us: call(): pl.pallas_call(kernel, out_shape=[jax.ShapeDtypeStruct(shape, kind) for s...]
    sub x1 -> x0, other arithmetic: 6.53 us -> none  [per_device(): return factor - 0.5 * grad / rms]
    psum x1 -> x0, blocking collectives: 5.53 us -> none  [per_device(): total = lax.psum(jnp.sum(grad * grad), 'feat')]
  transfers between devices with their start and end apart: 2 -> 32, of which waited for: 2 -> 13; matrix products, arithmetic and copies ran while one was open for 0% -> 0% of each run, Pallas kernels for 0% -> 20%
where the time goes in v1:
time: 106 us
  waiting for transfers between devices  45.5 us (43%)
  starting transfers between devices  34.7 us (33%)
  Pallas kernels  23.7 us (22%)
  local copies, waits for them, and re-layouts  1.32 us (1%)
    ppermute x27, waiting for transfers between devices, swap(): return lax.ppermute(x, 'samples', [(i, i ^ bit) for i in range(n)])  39.7 us
    ppermute x27, starting transfers between devices, swap(): return lax.ppermute(x, 'samples', [(i, i ^ bit) for i in range(n)])  26.9 us
    pallas_call x15, Pallas kernels, call(): pl.pallas_call(kernel, out_shape=[jax.ShapeDtypeStruct(shape, kind) for s...  17.9 us
    ppermute x5, starting transfers between devices, across(): lax.ppermute(x, 'feat', [(i, (i + 1) % halves) for i in range(halves)])  7.83 us
    ppermute x5, waiting for transfers between devices, across(): lax.ppermute(x, 'feat', [(i, (i + 1) % halves) for i in range(halves)])  5.85 us
    pallas_call x2, Pallas kernels, update(): pl.pallas_call(functools.partial(update_kernel, places, fresh, entries, r...  5.82 us
  transfers between devices with their start and end apart: 32, of which 13 were waited for; matrix products, arithmetic and copies ran while one was open for 0% of the time, Pallas kernels for 20%

profile of v1, /device:TPU:0, one launch (start us, length us, event | category | flops | bytes accessed | tf_op | source)
XLA Modules:
  0.0 105.5 jit_solution(7355281973768221381)
XLA Ops:
  0.5 2.6 %shard_map.28 = (f32[256,128]{1,0:T(8,128)S(1)}, bf16[2048,256]{1,0:T(8,128)(2,1)S(1)}) custom-call(f32[256,2048]{1,0:T(8,128)} %samples_ref.2, f32[2048,512]{1,0:T(8,128)} %factor_ref.11), custom_call_target="tpu_custom_call" | custom-call | tf_op jit(solution)/shard_map/pallas_call | solution.py:231
  3.1 2.6 %collective-permute-start.1 = (f32[256,128]{1,0:T(8,128)S(1)}, f32[256,128]{1,0:T(8,128)S(1)}, u32[]{:S(2)}, u32[]{:S(2)}) collective-permute-start(f32[256,128]{1,0:T(8,128)S(1)} %get-tuple-element.43.refs_0_), channel_id=1, source_target_pairs={{0,1},{1,0},{2,3},{3,2},{4,5},{5,4},{6,7},{7,6},{8,9},{9,8},{10,11... | collective-permute-start | bytes 393224 | tf_op jit(solution)/shard_map/ppermute | solution.py:259
  6.9 2.3 %shard_map.29.refs_2_ = f32[256,128]{1,0:T(8,128)S(1)} custom-call(f32[256,2048]{1,0:T(8,128)} %copy-done, bf16[2048,256]{1,0:T(8,128)(2,1)S(1)} %get-tuple-element.29.pair_ref), custom_call_target="tpu_custom_call" | custom-call | tf_op jit(solution)/shard_map/pallas_call | solution.py:231
  11.0 2.6 %shard_map.30 = (f32[256,128]{1,0:T(8,128)S(1)}, bf16[2048,256]{1,0:T(8,128)(2,1)S(1)}, bf16[2048,256]{1,0:T(8,128)(2,1)S(1)}, bf16[2048,256]{1,0:T(8,128)(2,1)S(1)}, bf16[256,2048]{1,0:T(8,128)(2,1)S(1)}) custom-call(f32[256,2048]{1,0:T(8,128)} %samples_ref.2, f32[2048,512]{1,0:T(8,128)} %factor_ref.11), custom_call_target="tpu_custom_call" | custom-call | tf_op jit(solution)/shard_map/pallas_call | solution.py:231
  13.6 2.3 %shard_map.31 = (f32[512,128]{1,0:T(8,128)S(1)}, bf16[2048,256]{1,0:T(8,128)(2,1)S(1)}, bf16[2048,256]{1,0:T(8,128)(2,1)S(1)}) custom-call(f32[256,2048]{1,0:T(8,128)} %copy-done, bf16[2048,256]{1,0:T(8,128)(2,1)S(1)} %get-tuple-element.32.pair_ref, f32[256,128]{1,0:T(8,128)S(1)} %get-tuple-element.33.own_ref), custom_call_target="tpu_custom_call" | custom-call | tf_op jit(solution)/shard_map/pallas_call | solution.py:231
  16.8 1.8 %collective-permute-start.7 = (f32[512,128]{1,0:T(8,128)S(1)}, f32[512,128]{1,0:T(8,128)S(1)}, u32[]{:S(2)}, u32[]{:S(2)}) collective-permute-start(f32[512,128]{1,0:T(8,128)S(1)} %shard_map.32), channel_id=1, source_target_pairs={{0,4},{2,6},{4,0},{6,2},{8,12},{10,14},{12,8},{14,10},{16,20},{18,... | collective-permute-start | bytes 786440 | tf_op jit(solution)/shard_map/ppermute | solution.py:256
  20.3 3.8 %collective-permute-done.3.refs_1_ = f32[512,128]{1,0:T(8,128)S(1)} collective-permute-done((f32[512,128]{1,0:T(8,128)S(1)}, f32[512,128]{1,0:T(8,128)S(1)}, u32[]{:S(2)}, u32[]{:S(2)}) %collective-permute-start.3) | collective-permute-done | bytes 262176 | tf_op jit(solution)/shard_map/ppermute | solution.py:259
  26.0 1.9 %collective-permute-start.8 = (f32[512,128]{1,0:T(8,128)S(1)}, f32[512,128]{1,0:T(8,128)S(1)}, u32[]{:S(2)}, u32[]{:S(2)}) collective-permute-start(f32[512,128]{1,0:T(8,128)S(1)} %add.24), channel_id=1, source_target_pairs={{0,8},{2,10},{4,12},{6,14},{8,0},{10,2},{12,4},{14,6},{16,24},{18,... | collective-permute-start | bytes 786440 | tf_op jit(solution)/shard_map/ppermute | solution.py:256
  31.3 2.6 %shard_map.40.a_ref = f32[128,512]{1,0:T(8,128)S(1)} custom-call(f32[2048,512]{1,0:T(8,128)} %factor_ref.11, bf16[256,2048]{1,0:T(8,128)(2,1)S(1)} %get-tuple-element.48.turned_ref), custom_call_target="tpu_custom_call" | custom-call | tf_op jit(solution)/shard_map/pallas_call | solution.py:231
  37.3 1.9 %collective-permute-start.11 = (f32[512,128]{1,0:T(8,128)S(1)}, f32[512,128]{1,0:T(8,128)S(1)}, u32[]{:S(2)}, u32[]{:S(2)}) collective-permute-start(f32[512,128]{1,0:T(8,128)S(1)} %add.27), channel_id=1, source_target_pairs={{0,8},{2,10},{4,12},{6,14},{8,0},{10,2},{12,4},{14,6},{16,24},{18,... | collective-permute-start | bytes 786440 | tf_op jit(solution)/shard_map/ppermute | solution.py:256
  39.2 2.6 %collective-permute-start.9 = (f32[512,128]{1,0:T(8,128)S(1)}, f32[512,128]{1,0:T(8,128)S(1)}, u32[]{:S(2)}, u32[]{:S(2)}) collective-permute-start(f32[512,128]{1,0:T(8,128)S(1)} %add_add_fusion), channel_id=1, source_target_pairs={{0,16},{2,18},{4,20},{6,22},{8,24},{10,26},{12,28},{14,30},{16,0},... | collective-permute-start | bytes 786440 | tf_op jit(solution)/shard_map/ppermute | solution.py:256
  43.5 5.0 %collective-permute-done.11.refs_3_ = f32[512,128]{1,0:T(8,128)S(1)} collective-permute-done((f32[512,128]{1,0:T(8,128)S(1)}, f32[512,128]{1,0:T(8,128)S(1)}, u32[]{:S(2)}, u32[]{:S(2)}) %collective-permute-start.11) | collective-permute-done | bytes 262176 | tf_op jit(solution)/shard_map/ppermute | solution.py:256
  48.5 5.4 %collective-permute-done.9.refs_2_ = f32[512,128]{1,0:T(8,128)S(1)} collective-permute-done((f32[512,128]{1,0:T(8,128)S(1)}, f32[512,128]{1,0:T(8,128)S(1)}, u32[]{:S(2)}, u32[]{:S(2)}) %collective-permute-start.9) | collective-permute-done | bytes 262176 | tf_op jit(solution)/shard_map/ppermute | solution.py:256
  54.2 4.2 %collective-permute-start.25 = (f32[512,128]{1,0:T(8,128)S(1)}, f32[512,128]{1,0:T(8,128)S(1)}, u32[]{:S(2)}, u32[]{:S(2)}) collective-permute-start(f32[512,128]{1,0:T(8,128)S(1)} %get-tuple-element.52.refs_0_), channel_id=1, source_target_pairs={{0,8},{2,10},{4,12},{6,14},{8,0},{10,2},{12,4},{14,6},{16,24},{18,... | collective-permute-start | bytes 786440 | tf_op jit(solution)/shard_map/ppermute | solution.py:256
  59.9 4.5 %collective-permute-done.17.refs_8_ = f32[512,128]{1,0:T(8,128)S(1)} collective-permute-done((f32[512,128]{1,0:T(8,128)S(1)}, f32[512,128]{1,0:T(8,128)S(1)}, u32[]{:S(2)}, u32[]{:S(2)}) %collective-permute-start.17) | collective-permute-done | bytes 262176 | tf_op jit(solution)/shard_map/ppermute | solution.py:256
  65.9 2.0 %collective-permute-done.12 = f32[8,128]{1,0:T(8,128)S(1)} collective-permute-done((f32[8,128]{1,0:T(8,128)S(1)}, f32[8,128]{1,0:T(8,128)S(1)}, u32[]{:S(2)}, u32[]{:S(2)}) %collective-permute-start.12) | collective-permute-done | bytes 4128 | tf_op jit(solution)/shard_map/ppermute | solution.py:259
  69.4 3.0 %collective-permute-done.13 = f32[8,128]{1,0:T(8,128)S(1)} collective-permute-done((f32[8,128]{1,0:T(8,128)S(1)}, f32[8,128]{1,0:T(8,128)S(1)}, u32[]{:S(2)}, u32[]{:S(2)}) %collective-permute-start.13) | collective-permute-done | bytes 4128 | tf_op jit(solution)/shard_map/ppermute | solution.py:256
  72.5 2.0 %collective-permute-start.14 = (f32[8,128]{1,0:T(8,128)S(1)}, f32[8,128]{1,0:T(8,128)S(1)}, u32[]{:S(2)}, u32[]{:S(2)}) collective-permute-start(f32[8,128]{1,0:T(8,128)S(1)} %add.29), channel_id=1, source_target_pairs={{0,8},{2,10},{4,12},{6,14},{8,0},{10,2},{12,4},{14,6},{16,24},{18,... | collective-permute-start | bytes 12296 | tf_op jit(solution)/shard_map/ppermute | solution.py:256
  77.7 2.0 %collective-permute-done.15 = f32[8,128]{1,0:T(8,128)S(1)} collective-permute-done((f32[8,128]{1,0:T(8,128)S(1)}, f32[8,128]{1,0:T(8,128)S(1)}, u32[]{:S(2)}, u32[]{:S(2)}) %collective-permute-start.15) | collective-permute-done | bytes 4128 | tf_op jit(solution)/shard_map/ppermute | solution.py:256
  83.7 5.3 %collective-permute-done.27.refs_6_ = f32[512,128]{1,0:T(8,128)S(1)} collective-permute-done((f32[512,128]{1,0:T(8,128)S(1)}, f32[512,128]{1,0:T(8,128)S(1)}, u32[]{:S(2)}, u32[]{:S(2)}) %collective-permute-start.27) | collective-permute-done | bytes 262176 | tf_op jit(solution)/shard_map/ppermute | solution.py:256
  89.5 5.1 %collective-permute-done.30.refs_10_ = f32[512,128]{1,0:T(8,128)S(1)} collective-permute-done((f32[512,128]{1,0:T(8,128)S(1)}, f32[512,128]{1,0:T(8,128)S(1)}, u32[]{:S(2)}, u32[]{:S(2)}) %collective-permute-start.30) | collective-permute-done | bytes 262176 | tf_op jit(solution)/shard_map/ppermute | solution.py:256
  95.1 4.6 %collective-permute-done.20.refs_2_ = f32[512,128]{1,0:T(8,128)S(1)} collective-permute-done((f32[512,128]{1,0:T(8,128)S(1)}, f32[512,128]{1,0:T(8,128)S(1)}, u32[]{:S(2)}, u32[]{:S(2)}) %collective-permute-start.20) | collective-permute-done | bytes 262176 | tf_op jit(solution)/shard_map/ppermute | solution.py:256
  99.7 3.3 %update.2.refs_4_ = f32[2048,512]{1,0:T(8,128)} custom-call(f32[8,128]{1,0:T(8,128)S(1)} %add.31.sums_a, f32[8,128]{1,0:T(8,128)S(1)} %collective-permute-done.16.sums_b, f32[2048,512]{1,0:T(8,128)} %factor_ref.11, f32[512,128]{1,0:T(8,128)S(1)} %get-tuple-element.52.refs_0_, f32[512,128]{1,0:T(8,128)S(1)} %collective-permute-done.22.refs_1_, ...), custom_call_target="tpu_custom_call" | custom-call | tf_op jit(solution)/shard_map/update/pallas_call | solution.py:210
  103.0 2.5 %update.3 = f32[2048,512]{1,0:T(8,128)} custom-call(f32[8,128]{1,0:T(8,128)S(1)} %add.31.sums_a, f32[8,128]{1,0:T(8,128)S(1)} %collective-permute-done.16.sums_b, f32[2048,512]{1,0:T(8,128)} %factor_ref.11, f32[512,128]{1,0:T(8,128)S(1)} %collective-permute-done.18.refs_0_, ...), custom_call_target="tpu_custom_call", output_to_operand_aliasing={{}: (7, {})} | custom-call | tf_op jit(solution)/shard_map/update/pallas_call | solution.py:210
  (66 shorter events, 29.5 us)
Async XLA Ops:
  3.1 13.3 %collective-permute-start.1 = (f32[256,128]{1,0:T(8,128)S(1)}, f32[256,128]{1,0:T(8,128)S(1)}, u32[]{:S(2)}, u32[]{:S(2)}) collective-permute-start(f32[256,128]{1,0:T(8,128)S(1)} %get-tuple-element.43.refs_0_), channel_id=1, source_target_pairs={{0,1},{1,0},{2,3},{3,2},{4,5},{5,4},{6,7},{7,6},{8,9},{9,8},{10,11... | collective-permute-start | bytes 393224 | tf_op jit(solution)/shard_map/ppermute | solution.py:259
  9.3 7.1 %collective-permute-start.2 = (f32[256,128]{1,0:T(8,128)S(1)}, f32[256,128]{1,0:T(8,128)S(1)}, u32[]{:S(2)}, u32[]{:S(2)}) collective-permute-start(f32[256,128]{1,0:T(8,128)S(1)} %shard_map.29.refs_2_), channel_id=1, source_target_pairs={{0,1},{1,0},{2,3},{3,2},{4,5},{5,4},{6,7},{7,6},{8,9},{9,8},{10,11... | collective-permute-start | bytes 393224 | tf_op jit(solution)/shard_map/ppermute | solution.py:259
  15.9 8.1 %collective-permute-start.3 = (f32[512,128]{1,0:T(8,128)S(1)}, f32[512,128]{1,0:T(8,128)S(1)}, u32[]{:S(2)}, u32[]{:S(2)}) collective-permute-start(f32[512,128]{1,0:T(8,128)S(1)} %get-tuple-element.47.refs_0_), channel_id=1, source_target_pairs={{0,1},{1,0},{2,3},{3,2},{4,5},{5,4},{6,7},{7,6},{8,9},{9,8},{10,11... | collective-permute-start | bytes 786440 | tf_op jit(solution)/shard_map/ppermute | solution.py:259
  16.8 9.2 %collective-permute-start.7 = (f32[512,128]{1,0:T(8,128)S(1)}, f32[512,128]{1,0:T(8,128)S(1)}, u32[]{:S(2)}, u32[]{:S(2)}) collective-permute-start(f32[512,128]{1,0:T(8,128)S(1)} %shard_map.32), channel_id=1, source_target_pairs={{0,4},{2,6},{4,0},{6,2},{8,12},{10,14},{12,8},{14,10},{16,20},{18,... | collective-permute-start | bytes 786440 | tf_op jit(solution)/shard_map/ppermute | solution.py:256
  19.0 16.4 %collective-permute-start.6 = (f32[512,128]{1,0:T(8,128)S(1)}, f32[512,128]{1,0:T(8,128)S(1)}, u32[]{:S(2)}, u32[]{:S(2)}) collective-permute-start(f32[512,128]{1,0:T(8,128)S(1)} %shard_map.33), channel_id=1, source_target_pairs={{0,4},{2,6},{4,0},{6,2},{8,12},{10,14},{12,8},{14,10},{16,20},{18,... | collective-permute-start | bytes 786440 | tf_op jit(solution)/shard_map/ppermute | solution.py:256
  26.0 9.4 %collective-permute-start.8 = (f32[512,128]{1,0:T(8,128)S(1)}, f32[512,128]{1,0:T(8,128)S(1)}, u32[]{:S(2)}, u32[]{:S(2)}) collective-permute-start(f32[512,128]{1,0:T(8,128)S(1)} %add.24), channel_id=1, source_target_pairs={{0,8},{2,10},{4,12},{6,14},{8,0},{10,2},{12,4},{14,6},{16,24},{18,... | collective-permute-start | bytes 786440 | tf_op jit(solution)/shard_map/ppermute | solution.py:256
  27.9 9.3 %collective-permute-start.10 = (f32[512,128]{1,0:T(8,128)S(1)}, f32[512,128]{1,0:T(8,128)S(1)}, u32[]{:S(2)}, u32[]{:S(2)}) collective-permute-start(f32[512,128]{1,0:T(8,128)S(1)} %shard_map.34), channel_id=1, source_target_pairs={{0,4},{2,6},{4,0},{6,2},{8,12},{10,14},{12,8},{14,10},{16,20},{18,... | collective-permute-start | bytes 786440 | tf_op jit(solution)/shard_map/ppermute | solution.py:256
  29.5 14.0 %collective-permute-start.5 = (f32[512,128]{1,0:T(8,128)S(1)}, f32[512,128]{1,0:T(8,128)S(1)}, u32[]{:S(2)}, u32[]{:S(2)}) collective-permute-start(f32[512,128]{1,0:T(8,128)S(1)} %shard_map.35), channel_id=1, source_target_pairs={{0,4},{2,6},{4,0},{6,2},{8,12},{10,14},{12,8},{14,10},{16,20},{18,... | collective-permute-start | bytes 786440 | tf_op jit(solution)/shard_map/ppermute | solution.py:256
  33.9 7.9 %collective-permute-start.4 = (f32[128,512]{1,0:T(8,128)S(1)}, f32[128,512]{1,0:T(8,128)S(1)}, u32[]{:S(2)}, u32[]{:S(2)}) collective-permute-start(f32[128,512]{1,0:T(8,128)S(1)} %shard_map.40.a_ref), channel_id=1, source_target_pairs={{0,1},{1,0},{2,3},{3,2},{4,5},{5,4},{6,7},{7,6},{8,9},{9,8},{10,11... | collective-permute-start | bytes 786440 | tf_op jit(solution)/shard_map/ppermute | solution.py:259
  37.3 11.3 %collective-permute-start.11 = (f32[512,128]{1,0:T(8,128)S(1)}, f32[512,128]{1,0:T(8,128)S(1)}, u32[]{:S(2)}, u32[]{:S(2)}) collective-permute-start(f32[512,128]{1,0:T(8,128)S(1)} %add.27), channel_id=1, source_target_pairs={{0,8},{2,10},{4,12},{6,14},{8,0},{10,2},{12,4},{14,6},{16,24},{18,... | collective-permute-start | bytes 786440 | tf_op jit(solution)/shard_map/ppermute | solution.py:256
  39.2 14.7 %collective-permute-start.9 = (f32[512,128]{1,0:T(8,128)S(1)}, f32[512,128]{1,0:T(8,128)S(1)}, u32[]{:S(2)}, u32[]{:S(2)}) collective-permute-start(f32[512,128]{1,0:T(8,128)S(1)} %add_add_fusion), channel_id=1, source_target_pairs={{0,16},{2,18},{4,20},{6,22},{8,24},{10,26},{12,28},{14,30},{16,0},... | collective-permute-start | bytes 786440 | tf_op jit(solution)/shard_map/ppermute | solution.py:256
  54.2 10.2 %collective-permute-start.17 = (f32[512,128]{1,0:T(8,128)S(1)}, f32[512,128]{1,0:T(8,128)S(1)}, u32[]{:S(2)}, u32[]{:S(2)}) collective-permute-start(f32[512,128]{1,0:T(8,128)S(1)} %get-tuple-element.52.refs_0_), channel_id=1, source_target_pairs={{0,16},{2,18},{4,20},{6,22},{8,24},{10,26},{12,28},{14,30},{16,0},... | collective-permute-start | bytes 786440 | tf_op jit(solution)/shard_map/ppermute | solution.py:256
  54.2 25.5 %collective-permute-start.25 = (f32[512,128]{1,0:T(8,128)S(1)}, f32[512,128]{1,0:T(8,128)S(1)}, u32[]{:S(2)}, u32[]{:S(2)}) collective-permute-start(f32[512,128]{1,0:T(8,128)S(1)} %get-tuple-element.52.refs_0_), channel_id=1, source_target_pairs={{0,8},{2,10},{4,12},{6,14},{8,0},{10,2},{12,4},{14,6},{16,24},{18,... | collective-permute-start | bytes 786440 | tf_op jit(solution)/shard_map/ppermute | solution.py:256
  58.4 23.2 %collective-permute-start.23 = (f32[512,128]{1,0:T(8,128)S(1)}, f32[512,128]{1,0:T(8,128)S(1)}, u32[]{:S(2)}, u32[]{:S(2)}) collective-permute-start(f32[512,128]{1,0:T(8,128)S(1)} %get-tuple-element.52.refs_0_), channel_id=1, source_target_pairs={{0,4},{2,6},{4,0},{6,2},{8,12},{10,14},{12,8},{14,10},{16,20},{18,... | collective-permute-start | bytes 786440 | tf_op jit(solution)/shard_map/ppermute | solution.py:256
  59.9 22.8 %collective-permute-start.22 = (f32[512,128]{1,0:T(8,128)S(1)}, f32[512,128]{1,0:T(8,128)S(1)}, u32[]{:S(2)}, u32[]{:S(2)}) collective-permute-start(f32[512,128]{1,0:T(8,128)S(1)} %get-tuple-element.52.refs_0_), channel_id=1, source_target_pairs={{0,2},{2,0},{4,6},{6,4},{8,10},{10,8},{12,14},{14,12},{16,18},{18,... | collective-permute-start | bytes 786440 | tf_op jit(solution)/shard_map/ppermute | solution.py:256
  64.4 18.4 %collective-permute-start.18 = (f32[512,128]{1,0:T(8,128)S(1)}, f32[512,128]{1,0:T(8,128)S(1)}, u32[]{:S(2)}, u32[]{:S(2)}) collective-permute-start(f32[512,128]{1,0:T(8,128)S(1)} %collective-permute-done.17.refs_8_), channel_id=1, source_target_pairs={{0,8},{2,10},{4,12},{6,14},{8,0},{10,2},{12,4},{14,6},{16,24},{18,... | collective-permute-start | bytes 786440 | tf_op jit(solution)/shard_map/ppermute | solution.py:256
  79.7 9.2 %collective-permute-start.27 = (f32[512,128]{1,0:T(8,128)S(1)}, f32[512,128]{1,0:T(8,128)S(1)}, u32[]{:S(2)}, u32[]{:S(2)}) collective-permute-start(f32[512,128]{1,0:T(8,128)S(1)} %collective-permute-done.25.refs_4_), channel_id=1, source_target_pairs={{0,4},{2,6},{4,0},{6,2},{8,12},{10,14},{12,8},{14,10},{16,20},{18,... | collective-permute-start | bytes 786440 | tf_op jit(solution)/shard_map/ppermute | solution.py:256
  81.4 7.6 %collective-permute-start.26 = (f32[512,128]{1,0:T(8,128)S(1)}, f32[512,128]{1,0:T(8,128)S(1)}, u32[]{:S(2)}, u32[]{:S(2)}) collective-permute-start(f32[512,128]{1,0:T(8,128)S(1)} %collective-permute-done.25.refs_4_), channel_id=1, source_target_pairs={{0,2},{2,0},{4,6},{6,4},{8,10},{10,8},{12,14},{14,12},{16,18},{18,... | collective-permute-start | bytes 786440 | tf_op jit(solution)/shard_map/ppermute | solution.py:256
  81.6 13.0 %collective-permute-start.30 = (f32[512,128]{1,0:T(8,128)S(1)}, f32[512,128]{1,0:T(8,128)S(1)}, u32[]{:S(2)}, u32[]{:S(2)}) collective-permute-start(f32[512,128]{1,0:T(8,128)S(1)} %collective-permute-done.17.refs_8_), channel_id=1, source_target_pairs={{0,4},{2,6},{4,0},{6,2},{8,12},{10,14},{12,8},{14,10},{16,20},{18,... | collective-permute-start | bytes 786440 | tf_op jit(solution)/shard_map/ppermute | solution.py:256
  82.7 11.9 %collective-permute-start.24 = (f32[512,128]{1,0:T(8,128)S(1)}, f32[512,128]{1,0:T(8,128)S(1)}, u32[]{:S(2)}, u32[]{:S(2)}) collective-permute-start(f32[512,128]{1,0:T(8,128)S(1)} %collective-permute-done.23.refs_2_), channel_id=1, source_target_pairs={{0,2},{2,0},{4,6},{6,4},{8,10},{10,8},{12,14},{14,12},{16,18},{18,... | collective-permute-start | bytes 786440 | tf_op jit(solution)/shard_map/ppermute | solution.py:256
  82.7 16.9 %collective-permute-start.20 = (f32[512,128]{1,0:T(8,128)S(1)}, f32[512,128]{1,0:T(8,128)S(1)}, u32[]{:S(2)}, u32[]{:S(2)}) collective-permute-start(f32[512,128]{1,0:T(8,128)S(1)} %collective-permute-done.18.refs_0_), channel_id=1, source_target_pairs={{0,4},{2,6},{4,0},{6,2},{8,12},{10,14},{12,8},{14,10},{16,20},{18,... | collective-permute-start | bytes 786440 | tf_op jit(solution)/shard_map/ppermute | solution.py:256
  89.0 10.7 %collective-permute-start.29 = (f32[512,128]{1,0:T(8,128)S(1)}, f32[512,128]{1,0:T(8,128)S(1)}, u32[]{:S(2)}, u32[]{:S(2)}) collective-permute-start(f32[512,128]{1,0:T(8,128)S(1)} %collective-permute-done.17.refs_8_), channel_id=1, source_target_pairs={{0,2},{2,0},{4,6},{6,4},{8,10},{10,8},{12,14},{14,12},{16,18},{18,... | collective-permute-start | bytes 786440 | tf_op jit(solution)/shard_map/ppermute | solution.py:256
  89.0 10.7 %collective-permute-start.28 = (f32[512,128]{1,0:T(8,128)S(1)}, f32[512,128]{1,0:T(8,128)S(1)}, u32[]{:S(2)}, u32[]{:S(2)}) collective-permute-start(f32[512,128]{1,0:T(8,128)S(1)} %collective-permute-done.27.refs_6_), channel_id=1, source_target_pairs={{0,2},{2,0},{4,6},{6,4},{8,10},{10,8},{12,14},{14,12},{16,18},{18,... | collective-permute-start | bytes 786440 | tf_op jit(solution)/shard_map/ppermute | solution.py:256
  94.6 8.4 %collective-permute-start.19 = (f32[512,128]{1,0:T(8,128)S(1)}, f32[512,128]{1,0:T(8,128)S(1)}, u32[]{:S(2)}, u32[]{:S(2)}) collective-permute-start(f32[512,128]{1,0:T(8,128)S(1)} %collective-permute-done.18.refs_0_), channel_id=1, source_target_pairs={{0,2},{2,0},{4,6},{6,4},{8,10},{10,8},{12,14},{14,12},{16,18},{18,... | collective-permute-start | bytes 786440 | tf_op jit(solution)/shard_map/ppermute | solution.py:256
  (9 other events, 32.4 us)

commit v2 on v1

v2 whole, which is shorter than its diff:
```python
import functools

import jax
import jax.numpy as jnp
from jax import lax
from jax.experimental import pallas as pl
from jax.experimental.pallas import tpu as pltpu
from jax.sharding import PartitionSpec as P


TILE = (8, 128)
CHUNKS = 4
WIDE, NARROW = jnp.float32, jnp.bfloat16


def after(x, *first):
    return lax.optimization_barrier((x,) + first)[0]


def position():
    me = lax.axis_index("samples")
    return me & 1, (me >> 1) & 1, me >> 2


def block(index, size):
    return pl.ds(pl.multiple_of(index * size, size), size)


def split(x):
    high = x.astype(NARROW)
    return high, (x - high.astype(WIDE)).astype(NARROW)


def matmul(a, b, contract=((1,), (0,))):
    return lax.dot_general(a, b, (contract, ((), ())), preferred_element_type=WIDE)


def three_pass(a_high, a_low, pair):
    cols = pair.shape[1] // 2
    wide = matmul(a_high, pair)
    return wide[:, :cols] + (wide[:, cols:] + matmul(a_low, pair[:, :cols]))


def fetch(source, held, sem):
    copy = pltpu.make_async_copy(source, held, sem)
    copy.start()
    return copy


def own_kernel(kept, samples_ref, factor_ref, *refs):
    proj_ref, pair_ref, *turned, held_x, held_f, sem = refs[kept:]
    core, y, _ = position()
    cols = proj_ref.shape[1]
    here = block(2 * core + (y if kept else 1 - y), cols)
    step = held_x.shape[1] // CHUNKS
    parts = [pl.ds(n * step, step) for n in range(CHUNKS)]
    copies = []
    for n, part in enumerate(parts):
        copies.append(fetch(factor_ref.at[part, here], held_f.at[part], sem.at[0, n]))
        copies.append(fetch(samples_ref.at[:, part], held_x.at[:, part], sem.at[1, n]))
    total = None
    for n, part in enumerate(parts):
        copies[2 * n].wait()
        pair = jnp.concatenate(split(held_f[part]), axis=1)
        pair_ref[part] = pair
        copies[2 * n + 1].wait()
        x = held_x[:, part]
        add = three_pass(*split(x), pair)
        total = add if total is None else total + add
        if kept:
            turned[0][part], turned[1][part] = split(x.T)
    proj_ref[...] = total


def other_kernel(samples_ref, pair_ref, proj_ref):
    proj_ref[...] = three_pass(*split(samples_ref[...]), pair_ref[...])


def both_kernel(samples_ref, pair_ref, own_ref, both_ref, high_ref, low_ref):
    count = own_ref.shape[0]
    x = samples_ref[...]
    both_ref[:count] = own_ref[...]
    both_ref[count:] = three_pass(*split(x), pair_ref[...])
    high_ref[...], low_ref[...] = split(x.T)


def moment_kernel(scale, starts, k, *refs):
    *projs, own_h, own_l, oth_h, oth_l, out_ref = refs
    rows, count = out_ref.shape[0], own_h.shape[1]
    here = block(position()[2] ^ k, rows)
    total = None
    for n, (h, l) in enumerate(((own_h, own_l), (oth_h, oth_l))):
        a, b = projs[2 * n : 2 * n + 2] if len(projs) == 4 else projs
        start = starts[n]
        proj = (a[start : start + count] + b[start : start + count]) * scale
        pair = jnp.concatenate(split(proj * proj), axis=1)
        part = three_pass(h[here, :], l[here, :], pair)
        total = part if total is None else total + part
    out_ref[...] = total


def gram_kernel(factor_ref, _, out_ref, held, sem):
    core, y, _ = position()
    cols = out_ref.shape[0]
    here = block(2 * core + y, cols)
    step = held.shape[0] // CHUNKS
    parts = [pl.ds(n * step, step) for n in range(CHUNKS)]
    copies = [
        fetch(factor_ref.at[part], held.at[part], sem.at[n]) for n, part in enumerate(parts)
    ]
    total = None
    for part, copy in zip(parts, copies):
        copy.wait()
        high, low = split(held[part])
        left = jnp.concatenate(split(held[part, here].T), axis=0)
        tall = matmul(left, high)
        add = tall[:cols] + (tall[cols:] + matmul(left[:cols], low))
        total = add if total is None else total + add
    out_ref[...] = total


def term_kernel(scale, factor_ref, a_ref, b_ref, out_ref, held, sem):
    fetch(factor_ref.at[block(position()[2], held.shape[0])], held, sem).wait()
    gram = (a_ref[...] + b_ref[...]) * (scale * scale)
    cols = gram.shape[0]
    tall = jnp.concatenate(split(gram * gram), axis=0)
    high, low = split(held[...])
    nt = ((1,), (1,))
    wide = matmul(high, tall, nt)
    out_ref[...] = (
        wide[:, :cols] + (wide[:, cols:] + matmul(low, tall[:cols], nt))
    ) * scale


def add_kernel(*refs):
    *parts, out_ref = refs
    total = parts[0][...]
    for part in parts[1:]:
        total = total + part[...]
    out_ref[...] = total


def grad_kernel(coef, total_rows, term_ref, *refs):
    *parts, grad_ref, sums_ref = refs
    total = parts[0][...]
    for part in parts[1:]:
        total = total + part[...]
    grad = coef * (term_ref[...] - total / total_rows)
    grad_ref[...] = grad
    down = jnp.sum(grad * grad, axis=0, keepdims=True)
    sums_ref[...] = jnp.broadcast_to(jnp.sum(down, axis=1, keepdims=True), sums_ref.shape)


def step_of(sums_a, sums_b, entries):
    rms = jnp.sqrt((sums_a[...] + sums_b[...]) / entries) + 1e-06
    return (0.5 / rms)[0:1, 0:1]


def columns_at(place, cols):
    core, y, _ = position()
    return block(2 * (core ^ place[2]) + (y ^ place[1]), cols)


def early_kernel(places, late, entries, rows, cols, sums_a, sums_b, factor_ref, *refs):
    count = len(places)
    blocks = refs[:count]
    out_ref, late_ref, held, got, in_sem, block_sem, out_sem = refs[count:]
    slabs = sorted({place[0] for place in places})

    def slab(k):
        return block(position()[2] ^ k, rows)

    loads = [fetch(factor_ref.at[slab(k)], held.at[s], in_sem.at[s]) for s, k in enumerate(slabs)]
    fetches = [fetch(blocks[b], got.at[b], block_sem.at[b]) for b in range(count)]
    step = step_of(sums_a, sums_b, entries)
    stores = []
    for s, k in enumerate(slabs):
        loads[s].wait()
        for b, place in enumerate(places):
            if place[0] == k:
                fetches[b].wait()
                here = columns_at(place, cols)
                held[s, :, here] = held[s, :, here] - step * got[b]
        for n, place in enumerate(late):
            if place[0] == k:
                late_ref[n] = held[s, :, columns_at(place, cols)]
        stores.append(fetch(held.at[s], out_ref.at[slab(k)], out_sem.at[s]))
    for store in stores:
        store.wait()


def late_kernel(places, entries, sums_a, sums_b, late_ref, *refs):
    count = len(places)
    blocks = refs[:count]
    _, out_ref, done, out_sem = refs[count:]
    step = step_of(sums_a, sums_b, entries)
    stores = []
    for b, place in enumerate(places):
        done[b] = late_ref[b] - step * blocks[b][...]
        rows, cols = blocks[b].shape
        at = (block(position()[2] ^ place[0], rows), columns_at(place, cols))
        stores.append(fetch(done.at[b], out_ref.at[at], out_sem.at[b]))
    for store in stores:
        store.wait()


def in_hbm(x):
    return pltpu.with_memory_space_constraint(x, pltpu.HBM)


VMEM, HBM = pl.BlockSpec(memory_space=pltpu.VMEM), pl.BlockSpec(memory_space=pltpu.HBM)


def early_update(places, late, sums, factor, blocks, entries):
    count, (rows, cols) = len(blocks), blocks[0].shape
    slabs = len({place[0] for place in places})
    return pl.pallas_call(
        functools.partial(early_kernel, places, late, entries, rows, cols),
        out_shape=[
            jax.ShapeDtypeStruct(factor.shape, WIDE),
            jax.ShapeDtypeStruct((len(late), rows, cols), WIDE),
        ],
        in_specs=[VMEM, VMEM, HBM] + [pl.BlockSpec(memory_space=pl.ANY)] * count,
        out_specs=[HBM, VMEM],
        scratch_shapes=[
            pltpu.VMEM((slabs, rows, factor.shape[1]), WIDE),
            pltpu.VMEM((count, rows, cols), WIDE),
            pltpu.SemaphoreType.DMA((slabs,)),
            pltpu.SemaphoreType.DMA((count,)),
            pltpu.SemaphoreType.DMA((slabs,)),
        ],
        compiler_params=pltpu.CompilerParams(vmem_limit_bytes=14 << 20),
        name="early",
    )(*sums, in_hbm(factor), *blocks)


def late_update(places, sums, late, blocks, out, entries):
    count = len(blocks)
    return pl.pallas_call(
        functools.partial(late_kernel, places, entries),
        out_shape=jax.ShapeDtypeStruct(out.shape, WIDE),
        in_specs=[VMEM] * (3 + count) + [HBM],
        out_specs=HBM,
        input_output_aliases={3 + count: 0},
        scratch_shapes=[
            pltpu.VMEM(late.shape, WIDE),
            pltpu.SemaphoreType.DMA((count,)),
        ],
        compiler_params=pltpu.CompilerParams(vmem_limit_bytes=8 << 20),
        name="late",
    )(*sums, late, *blocks, out)


def call(kernel, inputs, outputs, grant, hbm=(), scratch=()):
    return pl.pallas_call(
        kernel,
        out_shape=[jax.ShapeDtypeStruct(shape, kind) for shape, kind in outputs],
        in_specs=[HBM if i in hbm else VMEM for i in range(len(inputs))],
        out_specs=[VMEM] * len(outputs),
        scratch_shapes=list(scratch),
        compiler_params=pltpu.CompilerParams(vmem_limit_bytes=grant << 20),
    )(*[in_hbm(x) if i in hbm else x for i, x in enumerate(inputs)])


def low_bit(k):
    return k & -k


def gradient_step(samples, factor):
    features, rank = factor.shape
    count = samples.shape[0]
    n = lax.axis_size("samples")
    halves = lax.axis_size("feat")
    full = features * halves
    depth = n // 4
    rows = features // depth
    cols = rank // 4

    def swap(x, bit):
        return lax.ppermute(x, "samples", [(i, i ^ bit) for i in range(n)])

    def across(x):
        return lax.ppermute(x, "feat", [(i, (i + 1) % halves) for i in range(halves)])

    proj_of, pair_of = ((count, cols), WIDE), ((features, 2 * cols), NARROW)
    turned = ((features, count), NARROW)
    block_of = ((rows, cols), WIDE)
    held_x = [pltpu.VMEM(samples.shape, WIDE)]
    held_f = [pltpu.VMEM((features, cols), WIDE)]
    dmas = [pltpu.SemaphoreType.DMA((CHUNKS,))]
    two_dmas = [pltpu.SemaphoreType.DMA((2, CHUNKS))]

    other = swap(samples, 1)
    own_t, pair_t = call(
        functools.partial(own_kernel, False), [samples, factor], [proj_of, pair_of],
        12, (0, 1), held_x + held_f + two_dmas,
    )
    own_t2 = across(own_t)
    (oth_t,) = call(other_kernel, [other, pair_t], [proj_of], 8)
    oth_t2 = across(oth_t)
    own_m, pair_m, own_h, own_l = call(
        functools.partial(own_kernel, True), [samples, factor, oth_t],
        [proj_of, pair_of, turned, turned], 12, (0, 1), held_x + held_f + two_dmas,
    )
    both, oth_h, oth_l = call(
        both_kernel, [other, pair_m, own_m],
        [((2 * count, cols), WIDE), turned, turned], 10,
    )
    both2 = across(both)

    def moment_of(k, projs, starts):
        return call(
            functools.partial(moment_kernel, full**-0.5, starts, k),
            [*projs, own_h, own_l, oth_h, oth_l], [block_of], 8,
        )[0]

    order = range(depth - 1, -1, -1)
    arrived, kept = {}, {}
    for k in order:
        last = moment_of(k, [own_t, own_t2, oth_t, oth_t2], (0, 0))
        arrived[k] = swap(last, 2)
    for k in order:
        kept[k] = last = moment_of(k, [after(both, last), both2], (0, count))
    (gram,) = call(
        gram_kernel, [factor, last], [((cols, rank), WIDE)], 10, (0,),
        [pltpu.VMEM(factor.shape, WIDE)] + dmas,
    )
    (term,) = call(
        functools.partial(term_kernel, full**-0.5),
        [factor, gram, across(gram)], [block_of], 8, (0,),
        [pltpu.VMEM((rows, rank), WIDE), pltpu.SemaphoreType.DMA],
    )

    def sum_of(*parts):
        return call(add_kernel, parts, [(parts[0].shape, WIDE)], 4)[0]

    parts = {k: [kept[k], arrived[k]] for k in order}
    for k in order:
        if k:
            bit = low_bit(k)
            parts[k ^ bit].append(swap(sum_of(*parts[k]), 4 * bit))
    grad, sums = call(
        functools.partial(grad_kernel, 6.0 / full**0.5, count * n),
        [term, *parts[0]], [block_of, (TILE, WIDE)], 8,
    )
    sums = sum_of(sums, across(sums))
    bit = depth // 2
    while bit:
        sums = sum_of(sums, swap(sums, 4 * bit))
        bit //= 2
    sums = sum_of(sums, swap(sums, 2))
    sums = (sums, swap(sums, 1))

    held = {0: grad}
    bit = depth // 2
    while bit:
        for k in sorted(held):
            held[k ^ bit] = swap(held[k], 4 * bit)
        bit //= 2
    blocks, places = [], []
    for k in range(depth):
        for j, value in enumerate((held[k], swap(held[k], 2))):
            blocks += [value, swap(value, 1)]
            places += [(k, j, 0), (k, j, 1)]
    entries = full * rank
    out, late = early_update(places[:-2], places[-2:], sums, factor, blocks[:-2], entries)
    return late_update(places[-2:], sums, late, blocks[-2:], out, entries)


def solution(mesh):
    placed = (P("samples", "feat"), P("feat", None))
    return jax.shard_map(
        gradient_step, mesh=mesh, in_specs=placed, out_specs=P("feat", None), check_vma=False
    )
```

time: 106 us -> 102 us (0.962)
  Pallas kernels: 23.7 us -> 19.5 us
  local copies, waits for them, and re-layouts: 1.32 us -> 0 us
  starting transfers between devices: 34.7 us -> 35.9 us
    pallas_call x15 -> x22, Pallas kernels: 17.9 us -> 14.9 us  [call(): pl.pallas_call(kernel, out_shape=[jax.ShapeDtypeStruct(shape, kind) for s...]
    ppermute x27, waiting for transfers between devices: 39.7 us -> 42.1 us  [swap(): return lax.ppermute(x, 'samples', [(i, i ^ bit) for i in range(n)])]
    ppermute x5, waiting for transfers between devices: 5.85 us -> 4.09 us  [across(): lax.ppermute(x, 'feat', [(i, (i + 1) % halves) for i in range(halves)])]
    ppermute x27, starting transfers between devices: 26.9 us -> 28.2 us  [swap(): return lax.ppermute(x, 'samples', [(i, i ^ bit) for i in range(n)])]
    unnamed x2 -> x0, local copies, waits for them, and re-layouts: 1.32 us -> none
    pallas_call x2, Pallas kernels: 5.82 us -> 4.59 us  [the longest x1 3.69 us: early_update(): pl.pallas_call(functools.partial(early_kernel, places, late, entries, row...]
  transfers between devices with their start and end apart: 32 -> 32, of which waited for: 13 -> 15; matrix products, arithmetic and copies ran while one was open for 0% -> 0% of each run, Pallas kernels for 20% -> 18%
where the time goes in v2:
time: 102 us
  waiting for transfers between devices  46.1 us (45%)
  starting transfers between devices  35.9 us (35%)
  Pallas kernels  19.5 us (19%)
    ppermute x27, waiting for transfers between devices, swap(): return lax.ppermute(x, 'samples', [(i, i ^ bit) for i in range(n)])  42.1 us
    ppermute x27, starting transfers between devices, swap(): return lax.ppermute(x, 'samples', [(i, i ^ bit) for i in range(n)])  28.2 us
    pallas_call x22, Pallas kernels, call(): pl.pallas_call(kernel, out_shape=[jax.ShapeDtypeStruct(shape, kind) for s...  14.9 us
    ppermute x5, starting transfers between devices, across(): lax.ppermute(x, 'feat', [(i, (i + 1) % halves) for i in range(halves)])  7.73 us
    ppermute x5, waiting for transfers between devices, across(): lax.ppermute(x, 'feat', [(i, (i + 1) % halves) for i in range(halves)])  4.09 us
    pallas_call x1, Pallas kernels, early_update(): pl.pallas_call(functools.partial(early_kernel, places, late, entries, row...  3.69 us
  transfers between devices with their start and end apart: 32, of which 15 were waited for; matrix products, arithmetic and copies ran while one was open for 0% of the time, Pallas kernels for 18%

profile of v2, /device:TPU:0, one launch (start us, length us, event | category | flops | bytes accessed | tf_op | source)
XLA Modules:
  0.0 101.8 jit_solution(6111202528917104850)
XLA Ops:
  0.5 2.6 %shard_map.28 = (f32[256,128]{1,0:T(8,128)S(1)}, bf16[2048,256]{1,0:T(8,128)(2,1)S(1)}) custom-call(f32[256,2048]{1,0:T(8,128)} %samples_ref.3, f32[2048,512]{1,0:T(8,128)} %factor_ref.9), custom_call_target="tpu_custom_call" | custom-call | tf_op jit(solution)/shard_map/pallas_call | solution.py:255
  3.1 2.6 %collective-permute-start.1 = (f32[256,128]{1,0:T(8,128)S(1)}, f32[256,128]{1,0:T(8,128)S(1)}, u32[]{:S(2)}, u32[]{:S(2)}) collective-permute-start(f32[256,128]{1,0:T(8,128)S(1)} %get-tuple-element.26.refs_0_), channel_id=1, source_target_pairs={{0,1},{1,0},{2,3},{3,2},{4,5},{5,4},{6,7},{7,6},{8,9},{9,8},{10,11... | collective-permute-start | bytes 393224 | tf_op jit(solution)/shard_map/ppermute | solution.py:283
  6.3 1.8 %collective-permute-start.2 = (f32[256,128]{1,0:T(8,128)S(1)}, f32[256,128]{1,0:T(8,128)S(1)}, u32[]{:S(2)}, u32[]{:S(2)}) collective-permute-start(f32[256,128]{1,0:T(8,128)S(1)} %shard_map.29.refs_0_.refs_2_), channel_id=1, source_target_pairs={{0,1},{1,0},{2,3},{3,2},{4,5},{5,4},{6,7},{7,6},{8,9},{9,8},{10,11... | collective-permute-start | bytes 393224 | tf_op jit(solution)/shard_map/ppermute | solution.py:283
  8.1 2.6 %shard_map.30 = (f32[256,128]{1,0:T(8,128)S(1)}, bf16[2048,256]{1,0:T(8,128)(2,1)S(1)}, bf16[2048,256]{1,0:T(8,128)(2,1)S(1)}, bf16[2048,256]{1,0:T(8,128)(2,1)S(1)}) custom-call(f32[256,2048]{1,0:T(8,128)} %samples_ref.3, f32[2048,512]{1,0:T(8,128)} %factor_ref.9, f32[256,128]{1,0:T(8,128)S(1)} %shard_map.29.refs_0_.refs_2_), custom_call_target="tpu_custom_call" | custom-call | tf_op jit(solution)/shard_map/pallas_call | solution.py:255
  13.0 1.8 %collective-permute-start.7 = (f32[512,128]{1,0:T(8,128)S(1)}, f32[512,128]{1,0:T(8,128)S(1)}, u32[]{:S(2)}, u32[]{:S(2)}) collective-permute-start(f32[512,128]{1,0:T(8,128)S(1)} %shard_map.40), channel_id=1, source_target_pairs={{0,4},{2,6},{4,0},{6,2},{8,12},{10,14},{12,8},{14,10},{16,20},{18,... | collective-permute-start | bytes 786440 | tf_op jit(solution)/shard_map/ppermute | solution.py:280
  16.6 1.8 %collective-permute-start.10 = (f32[512,128]{1,0:T(8,128)S(1)}, f32[512,128]{1,0:T(8,128)S(1)}, u32[]{:S(2)}, u32[]{:S(2)}) collective-permute-start(f32[512,128]{1,0:T(8,128)S(1)} %shard_map.43), channel_id=1, source_target_pairs={{0,4},{2,6},{4,0},{6,2},{8,12},{10,14},{12,8},{14,10},{16,20},{18,... | collective-permute-start | bytes 786440 | tf_op jit(solution)/shard_map/ppermute | solution.py:280
  20.1 2.2 %collective-permute-done.7.refs_1_ = f32[512,128]{1,0:T(8,128)S(1)} collective-permute-done((f32[512,128]{1,0:T(8,128)S(1)}, f32[512,128]{1,0:T(8,128)S(1)}, u32[]{:S(2)}, u32[]{:S(2)}) %collective-permute-start.7) | collective-permute-done | bytes 262176 | tf_op jit(solution)/shard_map/ppermute | solution.py:280
  22.3 1.9 %collective-permute-start.8 = (f32[512,128]{1,0:T(8,128)S(1)}, f32[512,128]{1,0:T(8,128)S(1)}, u32[]{:S(2)}, u32[]{:S(2)}) collective-permute-start(f32[512,128]{1,0:T(8,128)S(1)} %shard_map.41), channel_id=1, source_target_pairs={{0,8},{2,10},{4,12},{6,14},{8,0},{10,2},{12,4},{14,6},{16,24},{18,... | collective-permute-start | bytes 786440 | tf_op jit(solution)/shard_map/ppermute | solution.py:280
  27.1 2.6 %shard_map.37.a_ref = f32[128,512]{1,0:T(8,128)S(1)} custom-call(f32[2048,512]{1,0:T(8,128)} %factor_ref.9, f32[512,128]{1,0:T(8,128)S(1)} %shard_map.36._.refs_0_), custom_call_target="tpu_custom_call" | custom-call | tf_op jit(solution)/shard_map/pallas_call | solution.py:255
  31.3 2.2 %collective-permute-done.10.refs_1_ = f32[512,128]{1,0:T(8,128)S(1)} collective-permute-done((f32[512,128]{1,0:T(8,128)S(1)}, f32[512,128]{1,0:T(8,128)S(1)}, u32[]{:S(2)}, u32[]{:S(2)}) %collective-permute-start.10) | collective-permute-done | bytes 262176 | tf_op jit(solution)/shard_map/ppermute | solution.py:280
  33.5 1.9 %collective-permute-start.11 = (f32[512,128]{1,0:T(8,128)S(1)}, f32[512,128]{1,0:T(8,128)S(1)}, u32[]{:S(2)}, u32[]{:S(2)}) collective-permute-start(f32[512,128]{1,0:T(8,128)S(1)} %shard_map.44), channel_id=1, source_target_pairs={{0,8},{2,10},{4,12},{6,14},{8,0},{10,2},{12,4},{14,6},{16,24},{18,... | collective-permute-start | bytes 786440 | tf_op jit(solution)/shard_map/ppermute | solution.py:280
  35.5 2.7 %collective-permute-start.9 = (f32[512,128]{1,0:T(8,128)S(1)}, f32[512,128]{1,0:T(8,128)S(1)}, u32[]{:S(2)}, u32[]{:S(2)}) collective-permute-start(f32[512,128]{1,0:T(8,128)S(1)} %shard_map.42), channel_id=1, source_target_pairs={{0,16},{2,18},{4,20},{6,22},{8,24},{10,26},{12,28},{14,30},{16,0},... | collective-permute-start | bytes 786440 | tf_op jit(solution)/shard_map/ppermute | solution.py:280
  39.9 5.4 %collective-permute-done.11.refs_3_ = f32[512,128]{1,0:T(8,128)S(1)} collective-permute-done((f32[512,128]{1,0:T(8,128)S(1)}, f32[512,128]{1,0:T(8,128)S(1)}, u32[]{:S(2)}, u32[]{:S(2)}) %collective-permute-start.11) | collective-permute-done | bytes 262176 | tf_op jit(solution)/shard_map/ppermute | solution.py:280
  45.2 5.3 %collective-permute-done.9.refs_2_ = f32[512,128]{1,0:T(8,128)S(1)} collective-permute-done((f32[512,128]{1,0:T(8,128)S(1)}, f32[512,128]{1,0:T(8,128)S(1)}, u32[]{:S(2)}, u32[]{:S(2)}) %collective-permute-start.9) | collective-permute-done | bytes 262176 | tf_op jit(solution)/shard_map/ppermute | solution.py:280
  50.8 4.3 %collective-permute-start.20 = (f32[512,128]{1,0:T(8,128)S(1)}, f32[512,128]{1,0:T(8,128)S(1)}, u32[]{:S(2)}, u32[]{:S(2)}) collective-permute-start(f32[512,128]{1,0:T(8,128)S(1)} %get-tuple-element.36.refs_0_), channel_id=1, source_target_pairs={{0,8},{2,10},{4,12},{6,14},{8,0},{10,2},{12,4},{14,6},{16,24},{18,... | collective-permute-start | bytes 786440 | tf_op jit(solution)/shard_map/ppermute | solution.py:280
  56.6 4.4 %collective-permute-done.24.refs_8_ = f32[512,128]{1,0:T(8,128)S(1)} collective-permute-done((f32[512,128]{1,0:T(8,128)S(1)}, f32[512,128]{1,0:T(8,128)S(1)}, u32[]{:S(2)}, u32[]{:S(2)}) %collective-permute-start.24) | collective-permute-done | bytes 262176 | tf_op jit(solution)/shard_map/ppermute | solution.py:280
  62.5 2.1 %collective-permute-done.12.refs_1_ = f32[8,128]{1,0:T(8,128)S(1)} collective-permute-done((f32[8,128]{1,0:T(8,128)S(1)}, f32[8,128]{1,0:T(8,128)S(1)}, u32[]{:S(2)}, u32[]{:S(2)}) %collective-permute-start.12) | collective-permute-done | bytes 4128 | tf_op jit(solution)/shard_map/ppermute | solution.py:283
  66.1 3.0 %collective-permute-done.13.refs_1_ = f32[8,128]{1,0:T(8,128)S(1)} collective-permute-done((f32[8,128]{1,0:T(8,128)S(1)}, f32[8,128]{1,0:T(8,128)S(1)}, u32[]{:S(2)}, u32[]{:S(2)}) %collective-permute-start.13) | collective-permute-done | bytes 4128 | tf_op jit(solution)/shard_map/ppermute | solution.py:280
  69.1 2.0 %collective-permute-start.14 = (f32[8,128]{1,0:T(8,128)S(1)}, f32[8,128]{1,0:T(8,128)S(1)}, u32[]{:S(2)}, u32[]{:S(2)}) collective-permute-start(f32[8,128]{1,0:T(8,128)S(1)} %shard_map.47.refs_0_), channel_id=1, source_target_pairs={{0,8},{2,10},{4,12},{6,14},{8,0},{10,2},{12,4},{14,6},{16,24},{18,... | collective-permute-start | bytes 12296 | tf_op jit(solution)/shard_map/ppermute | solution.py:280
  74.3 2.0 %collective-permute-done.15.refs_1_ = f32[8,128]{1,0:T(8,128)S(1)} collective-permute-done((f32[8,128]{1,0:T(8,128)S(1)}, f32[8,128]{1,0:T(8,128)S(1)}, u32[]{:S(2)}, u32[]{:S(2)}) %collective-permute-start.15) | collective-permute-done | bytes 4128 | tf_op jit(solution)/shard_map/ppermute | solution.py:280
  81.3 5.3 %collective-permute-done.26.refs_10_ = f32[512,128]{1,0:T(8,128)S(1)} collective-permute-done((f32[512,128]{1,0:T(8,128)S(1)}, f32[512,128]{1,0:T(8,128)S(1)}, u32[]{:S(2)}, u32[]{:S(2)}) %collective-permute-start.26) | collective-permute-done | bytes 262176 | tf_op jit(solution)/shard_map/ppermute | solution.py:280
  87.2 5.1 %collective-permute-done.22.refs_6_ = f32[512,128]{1,0:T(8,128)S(1)} collective-permute-done((f32[512,128]{1,0:T(8,128)S(1)}, f32[512,128]{1,0:T(8,128)S(1)}, u32[]{:S(2)}, u32[]{:S(2)}) %collective-permute-start.22) | collective-permute-done | bytes 262176 | tf_op jit(solution)/shard_map/ppermute | solution.py:280
  92.8 4.3 %collective-permute-done.30.refs_0_ = f32[512,128]{1,0:T(8,128)S(1)} collective-permute-done((f32[512,128]{1,0:T(8,128)S(1)}, f32[512,128]{1,0:T(8,128)S(1)}, u32[]{:S(2)}, u32[]{:S(2)}) %collective-permute-start.30) | collective-permute-done | bytes 262176 | tf_op jit(solution)/shard_map/ppermute | solution.py:280
  97.2 3.7 %early.1 = (f32[2048,512]{1,0:T(8,128)}, f32[2,512,128]{2,1,0:T(8,128)S(1)}) custom-call(f32[8,128]{1,0:T(8,128)S(1)} %shard_map.49.sums_a, f32[8,128]{1,0:T(8,128)S(1)} %collective-permute-done.16.sums_b, f32[2048,512]{1,0:T(8,128)} %factor_ref.9, f32[512,128]{1,0:T(8,128)S(1)} %get-tuple-element.36.refs_0_, ...), custom_call_target="tpu_custom_call" | custom-call | tf_op jit(solution)/shard_map/early/pallas_call | solution.py:217
  (64 shorter events, 27.9 us)
Async XLA Ops:
  0.0 5.6 %collective-permute-start = (f32[256,2048]{1,0:T(8,128)}, f32[256,2048]{1,0:T(8,128)S(1)}, u32[]{:S(2)}, u32[]{:S(2)}) collective-permute-start(f32[256,2048]{1,0:T(8,128)} %samples_ref.3), channel_id=1, source_target_pairs={{0,2},{2,0},{4,6},{6,4},{8,10},{10,8},{12,14},{14,12},{16,18},{18,... | collective-permute-start | bytes 6291464 | tf_op jit(solution)/shard_map/ppermute | solution.py:280
  3.1 8.8 %collective-permute-start.1 = (f32[256,128]{1,0:T(8,128)S(1)}, f32[256,128]{1,0:T(8,128)S(1)}, u32[]{:S(2)}, u32[]{:S(2)}) collective-permute-start(f32[256,128]{1,0:T(8,128)S(1)} %get-tuple-element.26.refs_0_), channel_id=1, source_target_pairs={{0,1},{1,0},{2,3},{3,2},{4,5},{5,4},{6,7},{7,6},{8,9},{9,8},{10,11... | collective-permute-start | bytes 393224 | tf_op jit(solution)/shard_map/ppermute | solution.py:283
  6.3 6.2 %collective-permute-start.2 = (f32[256,128]{1,0:T(8,128)S(1)}, f32[256,128]{1,0:T(8,128)S(1)}, u32[]{:S(2)}, u32[]{:S(2)}) collective-permute-start(f32[256,128]{1,0:T(8,128)S(1)} %shard_map.29.refs_0_.refs_2_), channel_id=1, source_target_pairs={{0,1},{1,0},{2,3},{3,2},{4,5},{5,4},{6,7},{7,6},{8,9},{9,8},{10,11... | collective-permute-start | bytes 393224 | tf_op jit(solution)/shard_map/ppermute | solution.py:283
  11.5 8.1 %collective-permute-start.3 = (f32[512,128]{1,0:T(8,128)S(1)}, f32[512,128]{1,0:T(8,128)S(1)}, u32[]{:S(2)}, u32[]{:S(2)}) collective-permute-start(f32[512,128]{1,0:T(8,128)S(1)} %get-tuple-element.34.refs_0_), channel_id=1, source_target_pairs={{0,1},{1,0},{2,3},{3,2},{4,5},{5,4},{6,7},{7,6},{8,9},{9,8},{10,11... | collective-permute-start | bytes 786440 | tf_op jit(solution)/shard_map/ppermute | solution.py:283
  13.0 9.2 %collective-permute-start.7 = (f32[512,128]{1,0:T(8,128)S(1)}, f32[512,128]{1,0:T(8,128)S(1)}, u32[]{:S(2)}, u32[]{:S(2)}) collective-permute-start(f32[512,128]{1,0:T(8,128)S(1)} %shard_map.40), channel_id=1, source_target_pairs={{0,4},{2,6},{4,0},{6,2},{8,12},{10,14},{12,8},{14,10},{16,20},{18,... | collective-permute-start | bytes 786440 | tf_op jit(solution)/shard_map/ppermute | solution.py:280
  15.8 19.7 %collective-permute-start.6 = (f32[512,128]{1,0:T(8,128)S(1)}, f32[512,128]{1,0:T(8,128)S(1)}, u32[]{:S(2)}, u32[]{:S(2)}) collective-permute-start(f32[512,128]{1,0:T(8,128)S(1)} %shard_map.39), channel_id=1, source_target_pairs={{0,4},{2,6},{4,0},{6,2},{8,12},{10,14},{12,8},{14,10},{16,20},{18,... | collective-permute-start | bytes 786440 | tf_op jit(solution)/shard_map/ppermute | solution.py:280
  16.6 16.9 %collective-permute-start.10 = (f32[512,128]{1,0:T(8,128)S(1)}, f32[512,128]{1,0:T(8,128)S(1)}, u32[]{:S(2)}, u32[]{:S(2)}) collective-permute-start(f32[512,128]{1,0:T(8,128)S(1)} %shard_map.43), channel_id=1, source_target_pairs={{0,4},{2,6},{4,0},{6,2},{8,12},{10,14},{12,8},{14,10},{16,20},{18,... | collective-permute-start | bytes 786440 | tf_op jit(solution)/shard_map/ppermute | solution.py:280
  22.3 13.1 %collective-permute-start.8 = (f32[512,128]{1,0:T(8,128)S(1)}, f32[512,128]{1,0:T(8,128)S(1)}, u32[]{:S(2)}, u32[]{:S(2)}) collective-permute-start(f32[512,128]{1,0:T(8,128)S(1)} %shard_map.41), channel_id=1, source_target_pairs={{0,8},{2,10},{4,12},{6,14},{8,0},{10,2},{12,4},{14,6},{16,24},{18,... | collective-permute-start | bytes 786440 | tf_op jit(solution)/shard_map/ppermute | solution.py:280
  24.2 15.7 %collective-permute-start.5 = (f32[512,128]{1,0:T(8,128)S(1)}, f32[512,128]{1,0:T(8,128)S(1)}, u32[]{:S(2)}, u32[]{:S(2)}) collective-permute-start(f32[512,128]{1,0:T(8,128)S(1)} %shard_map.32), channel_id=1, source_target_pairs={{0,4},{2,6},{4,0},{6,2},{8,12},{10,14},{12,8},{14,10},{16,20},{18,... | collective-permute-start | bytes 786440 | tf_op jit(solution)/shard_map/ppermute | solution.py:280
  29.7 8.4 %collective-permute-start.4 = (f32[128,512]{1,0:T(8,128)S(1)}, f32[128,512]{1,0:T(8,128)S(1)}, u32[]{:S(2)}, u32[]{:S(2)}) collective-permute-start(f32[128,512]{1,0:T(8,128)S(1)} %shard_map.37.a_ref), channel_id=1, source_target_pairs={{0,1},{1,0},{2,3},{3,2},{4,5},{5,4},{6,7},{7,6},{8,9},{9,8},{10,11... | collective-permute-start | bytes 786440 | tf_op jit(solution)/shard_map/ppermute | solution.py:283
  33.5 11.7 %collective-permute-start.11 = (f32[512,128]{1,0:T(8,128)S(1)}, f32[512,128]{1,0:T(8,128)S(1)}, u32[]{:S(2)}, u32[]{:S(2)}) collective-permute-start(f32[512,128]{1,0:T(8,128)S(1)} %shard_map.44), channel_id=1, source_target_pairs={{0,8},{2,10},{4,12},{6,14},{8,0},{10,2},{12,4},{14,6},{16,24},{18,... | collective-permute-start | bytes 786440 | tf_op jit(solution)/shard_map/ppermute | solution.py:280
  35.5 15.1 %collective-permute-start.9 = (f32[512,128]{1,0:T(8,128)S(1)}, f32[512,128]{1,0:T(8,128)S(1)}, u32[]{:S(2)}, u32[]{:S(2)}) collective-permute-start(f32[512,128]{1,0:T(8,128)S(1)} %shard_map.42), channel_id=1, source_target_pairs={{0,16},{2,18},{4,20},{6,22},{8,24},{10,26},{12,28},{14,30},{16,0},... | collective-permute-start | bytes 786440 | tf_op jit(solution)/shard_map/ppermute | solution.py:280
  50.8 10.2 %collective-permute-start.24 = (f32[512,128]{1,0:T(8,128)S(1)}, f32[512,128]{1,0:T(8,128)S(1)}, u32[]{:S(2)}, u32[]{:S(2)}) collective-permute-start(f32[512,128]{1,0:T(8,128)S(1)} %get-tuple-element.36.refs_0_), channel_id=1, source_target_pairs={{0,16},{2,18},{4,20},{6,22},{8,24},{10,26},{12,28},{14,30},{16,0},... | collective-permute-start | bytes 786440 | tf_op jit(solution)/shard_map/ppermute | solution.py:280
  50.8 28.3 %collective-permute-start.20 = (f32[512,128]{1,0:T(8,128)S(1)}, f32[512,128]{1,0:T(8,128)S(1)}, u32[]{:S(2)}, u32[]{:S(2)}) collective-permute-start(f32[512,128]{1,0:T(8,128)S(1)} %get-tuple-element.36.refs_0_), channel_id=1, source_target_pairs={{0,8},{2,10},{4,12},{6,14},{8,0},{10,2},{12,4},{14,6},{16,24},{18,... | collective-permute-start | bytes 786440 | tf_op jit(solution)/shard_map/ppermute | solution.py:280
  55.1 23.9 %collective-permute-start.18 = (f32[512,128]{1,0:T(8,128)S(1)}, f32[512,128]{1,0:T(8,128)S(1)}, u32[]{:S(2)}, u32[]{:S(2)}) collective-permute-start(f32[512,128]{1,0:T(8,128)S(1)} %get-tuple-element.36.refs_0_), channel_id=1, source_target_pairs={{0,4},{2,6},{4,0},{6,2},{8,12},{10,14},{12,8},{14,10},{16,20},{18,... | collective-permute-start | bytes 786440 | tf_op jit(solution)/shard_map/ppermute | solution.py:280
  56.6 23.0 %collective-permute-start.17 = (f32[512,128]{1,0:T(8,128)S(1)}, f32[512,128]{1,0:T(8,128)S(1)}, u32[]{:S(2)}, u32[]{:S(2)}) collective-permute-start(f32[512,128]{1,0:T(8,128)S(1)} %get-tuple-element.36.refs_0_), channel_id=1, source_target_pairs={{0,2},{2,0},{4,6},{6,4},{8,10},{10,8},{12,14},{14,12},{16,18},{18,... | collective-permute-start | bytes 786440 | tf_op jit(solution)/shard_map/ppermute | solution.py:280
  61.0 18.8 %collective-permute-start.28 = (f32[512,128]{1,0:T(8,128)S(1)}, f32[512,128]{1,0:T(8,128)S(1)}, u32[]{:S(2)}, u32[]{:S(2)}) collective-permute-start(f32[512,128]{1,0:T(8,128)S(1)} %collective-permute-done.24.refs_8_), channel_id=1, source_target_pairs={{0,8},{2,10},{4,12},{6,14},{8,0},{10,2},{12,4},{14,6},{16,24},{18,... | collective-permute-start | bytes 786440 | tf_op jit(solution)/shard_map/ppermute | solution.py:280
  77.5 9.2 %collective-permute-start.26 = (f32[512,128]{1,0:T(8,128)S(1)}, f32[512,128]{1,0:T(8,128)S(1)}, u32[]{:S(2)}, u32[]{:S(2)}) collective-permute-start(f32[512,128]{1,0:T(8,128)S(1)} %collective-permute-done.24.refs_8_), channel_id=1, source_target_pairs={{0,4},{2,6},{4,0},{6,2},{8,12},{10,14},{12,8},{14,10},{16,20},{18,... | collective-permute-start | bytes 786440 | tf_op jit(solution)/shard_map/ppermute | solution.py:280
  79.1 7.6 %collective-permute-start.25 = (f32[512,128]{1,0:T(8,128)S(1)}, f32[512,128]{1,0:T(8,128)S(1)}, u32[]{:S(2)}, u32[]{:S(2)}) collective-permute-start(f32[512,128]{1,0:T(8,128)S(1)} %collective-permute-done.24.refs_8_), channel_id=1, source_target_pairs={{0,2},{2,0},{4,6},{6,4},{8,10},{10,8},{12,14},{14,12},{16,18},{18,... | collective-permute-start | bytes 786440 | tf_op jit(solution)/shard_map/ppermute | solution.py:280
  79.1 13.2 %collective-permute-start.22 = (f32[512,128]{1,0:T(8,128)S(1)}, f32[512,128]{1,0:T(8,128)S(1)}, u32[]{:S(2)}, u32[]{:S(2)}) collective-permute-start(f32[512,128]{1,0:T(8,128)S(1)} %collective-permute-done.20.refs_4_), channel_id=1, source_target_pairs={{0,4},{2,6},{4,0},{6,2},{8,12},{10,14},{12,8},{14,10},{16,20},{18,... | collective-permute-start | bytes 786440 | tf_op jit(solution)/shard_map/ppermute | solution.py:280
  79.6 12.7 %collective-permute-start.21 = (f32[512,128]{1,0:T(8,128)S(1)}, f32[512,128]{1,0:T(8,128)S(1)}, u32[]{:S(2)}, u32[]{:S(2)}) collective-permute-start(f32[512,128]{1,0:T(8,128)S(1)} %collective-permute-done.20.refs_4_), channel_id=1, source_target_pairs={{0,2},{2,0},{4,6},{6,4},{8,10},{10,8},{12,14},{14,12},{16,18},{18,... | collective-permute-start | bytes 786440 | tf_op jit(solution)/shard_map/ppermute | solution.py:280
  79.8 17.3 %collective-permute-start.30 = (f32[512,128]{1,0:T(8,128)S(1)}, f32[512,128]{1,0:T(8,128)S(1)}, u32[]{:S(2)}, u32[]{:S(2)}) collective-permute-start(f32[512,128]{1,0:T(8,128)S(1)} %collective-permute-done.28.refs_12_), channel_id=1, source_target_pairs={{0,4},{2,6},{4,0},{6,2},{8,12},{10,14},{12,8},{14,10},{16,20},{18,... | collective-permute-start | bytes 786440 | tf_op jit(solution)/shard_map/ppermute | solution.py:280
  86.7 10.4 %collective-permute-start.19 = (f32[512,128]{1,0:T(8,128)S(1)}, f32[512,128]{1,0:T(8,128)S(1)}, u32[]{:S(2)}, u32[]{:S(2)}) collective-permute-start(f32[512,128]{1,0:T(8,128)S(1)} %collective-permute-done.18.refs_2_), channel_id=1, source_target_pairs={{0,2},{2,0},{4,6},{6,4},{8,10},{10,8},{12,14},{14,12},{16,18},{18,... | collective-permute-start | bytes 786440 | tf_op jit(solution)/shard_map/ppermute | solution.py:280
  86.7 10.4 %collective-permute-start.29 = (f32[512,128]{1,0:T(8,128)S(1)}, f32[512,128]{1,0:T(8,128)S(1)}, u32[]{:S(2)}, u32[]{:S(2)}) collective-permute-start(f32[512,128]{1,0:T(8,128)S(1)} %collective-permute-done.28.refs_12_), channel_id=1, source_target_pairs={{0,2},{2,0},{4,6},{6,4},{8,10},{10,8},{12,14},{14,12},{16,18},{18,... | collective-permute-start | bytes 786440 | tf_op jit(solution)/shard_map/ppermute | solution.py:280
  (8 other events, 29.9 us)
